TPU v7x, 768 devices: a whole 4x8x12 slice. The times are simulated.
768 devices in a mesh: curve: 96 (over z, y), near: 8 (over x, core).
Axes of the slice: x: 4, y: 8, z: 12, core: 2. Of those that a mesh axis runs over, the one named last changes fastest.
Arguments:
- primitive: float32 [6, 32, 294912], P(None, 'near', 'curve'), may hold values from -2 to 2, as said below
- conductivity: float32 [32, 294912], P('near', 'curve'), may hold values from 0.05 to 0.5
- new_owner: int32 [288], P('curve'), may hold values from 0 to 95, as said below
Outputs:
- regridded: float32 [96, 6, 32, 4096], P('curve', None, 'near')
Inputs may be any that keep to these rules, and one draw needn't show every extreme that they name: `primitive`: fields in order: density and pressure within 0.5 to 2, three velocity components within -2 to 2, tracer concentration within 0 to 1. `new_owner`: before the regrid box column b lies on curve segment b // 3. Its new owner is that segment, except that the first box column of a segment c >= 1 may go to c - 1. Some segment ends with 4 box columns and some with 2.
All inputs are finite; a program needn't handle non-finite values.
Results may differ from a plain program's by a relative error of at most 0.0003.
Values sent between devices are 32-bit elements; how exact they have to be, the bound alone decides.
A program may use at most 32 MiB of HBM per device.

v0:
```python
import jax
import jax.numpy as jnp
from jax import lax
from jax.sharding import PartitionSpec as P

BW = 32


GAMMA = 1.4
COURANT = 0.8


def extended_2(x, sides, width, wrap):
    for axis, dim in sides:
        devices, length = (lax.axis_size(axis), x.shape[dim])
        up = [(i, (i + 1) % devices) for i in range(devices if wrap else devices - 1)]
        down = [(j, i) for i, j in up]
        last = lax.slice_in_dim(x, length - width, length, axis=dim)
        first = lax.slice_in_dim(x, 0, width, axis=dim)
        before = lax.ppermute(last, axis, up)
        after = lax.ppermute(first, axis, down)
        x = jnp.concatenate([before, x, after], axis=dim)
    return x


def shifted(block, axis, distance):
    devices = range(lax.axis_size(axis))
    route = [(i - distance, i) for i in devices if i - distance in devices]
    return lax.ppermute(block, axis, route)


def to_conserved(prim):
    specific_weight_field = prim[0]
    velocity = prim[1:4]
    normal_stress_field = prim[4]
    momentum = specific_weight_field[None] * velocity
    energy = normal_stress_field / (GAMMA - 1.0) + 0.5 * specific_weight_field * jnp.sum(
        velocity * velocity, axis=0
    )
    tracer = specific_weight_field * prim[5]
    return jnp.concatenate(
        [specific_weight_field[None], momentum, energy[None], tracer[None]], axis=0
    )


def wave_bound(prim):
    sound = jnp.sqrt(GAMMA * prim[4] / prim[0])
    return jnp.abs(prim[1]) + jnp.abs(prim[2]) + jnp.abs(prim[3]) + 3.0 * sound


def roll_upper(values, ypos, ghost_layer_depth):
    return jnp.where(
        ypos == ghost_layer_depth - 1,
        jnp.roll(values, ghost_layer_depth - 1, axis=-1),
        jnp.roll(values, -1, axis=-1),
    )


def roll_lower(values, ypos, ghost_layer_depth):
    return jnp.where(
        ypos == 0, jnp.roll(values, 1 - ghost_layer_depth, axis=-1), jnp.roll(values, 1, axis=-1)
    )


def face_flux(
    lower_u, upper_u, lower_f, upper_f, lower_s, upper_s, lower_k, upper_k, lower_t, upper_t
):
    flux = 0.5 * (lower_f + upper_f) - 0.5 * jnp.maximum(lower_s, upper_s)[None] * (
        upper_u - lower_u
    )
    heat = 0.5 * (lower_k + upper_k) * (upper_t - lower_t)
    return flux.at[4].add(-heat)


def compute_rate(extended, ext_kappa, ghost_layer_depth):
    specific_weight_field = extended[0]
    velocity = extended[1:4] / specific_weight_field[None]
    kinetic = 0.5 * jnp.sum(extended[1:4] * velocity, axis=0)
    normal_stress_field = (GAMMA - 1.0) * (extended[4] - kinetic)
    sound = jnp.sqrt(GAMMA * normal_stress_field / specific_weight_field)
    thermal_state_kelvin = normal_stress_field / specific_weight_field

    def physical(direction):
        speed_dir = velocity[direction]
        fluxes = extended * speed_dir[None]
        fluxes = fluxes.at[1 + direction].add(normal_stress_field)
        fluxes = fluxes.at[4].add(normal_stress_field * speed_dir)
        return (fluxes, jnp.abs(speed_dir) + sound)

    fluxes, signal = physical(0)
    rows_u = extended[:, 1:-1]
    rows_f = fluxes[:, 1:-1]
    rows_s = signal[1:-1]
    rows_k = ext_kappa[1:-1]
    horizontal_line_number = thermal_state_kelvin[1:-1]
    faces = face_flux(
        rows_u[..., :-ghost_layer_depth],
        rows_u[..., ghost_layer_depth:],
        rows_f[..., :-ghost_layer_depth],
        rows_f[..., ghost_layer_depth:],
        rows_s[..., :-ghost_layer_depth],
        rows_s[..., ghost_layer_depth:],
        rows_k[..., :-ghost_layer_depth],
        rows_k[..., ghost_layer_depth:],
        horizontal_line_number[..., :-ghost_layer_depth],
        horizontal_line_number[..., ghost_layer_depth:],
    )
    total = faces[..., ghost_layer_depth:] - faces[..., :-ghost_layer_depth]
    fluxes, signal = physical(2)
    cols_u = extended[..., ghost_layer_depth:-ghost_layer_depth]
    cols_f = fluxes[..., ghost_layer_depth:-ghost_layer_depth]
    cols_s = signal[..., ghost_layer_depth:-ghost_layer_depth]
    cols_k = ext_kappa[..., ghost_layer_depth:-ghost_layer_depth]
    vertical_count_grid = thermal_state_kelvin[..., ghost_layer_depth:-ghost_layer_depth]
    faces = face_flux(
        cols_u[:, :-1],
        cols_u[:, 1:],
        cols_f[:, :-1],
        cols_f[:, 1:],
        cols_s[:-1],
        cols_s[1:],
        cols_k[:-1],
        cols_k[1:],
        vertical_count_grid[:-1],
        vertical_count_grid[1:],
    )
    total = total + faces[:, 1:] - faces[:, :-1]
    fluxes, signal = physical(1)
    inner_u = extended[:, 1:-1, ghost_layer_depth:-ghost_layer_depth]
    inner_f = fluxes[:, 1:-1, ghost_layer_depth:-ghost_layer_depth]
    inner_s = signal[1:-1, ghost_layer_depth:-ghost_layer_depth]
    inner_k = ext_kappa[1:-1, ghost_layer_depth:-ghost_layer_depth]
    core_cell_number = thermal_state_kelvin[1:-1, ghost_layer_depth:-ghost_layer_depth]
    ypos = jnp.arange(inner_u.shape[-1]) % ghost_layer_depth
    faces = face_flux(
        inner_u,
        roll_upper(inner_u, ypos, ghost_layer_depth),
        inner_f,
        roll_upper(inner_f, ypos, ghost_layer_depth),
        inner_s,
        roll_upper(inner_s, ypos, ghost_layer_depth),
        inner_k,
        roll_upper(inner_k, ypos, ghost_layer_depth),
        core_cell_number,
        roll_upper(core_cell_number, ypos, ghost_layer_depth),
    )
    total = total + faces - roll_lower(faces, ypos, ghost_layer_depth)
    return -total


def section_rate(state, kappa, box_count, segment, segments):
    ghost_layer_depth = BW
    box_cells = ghost_layer_depth * ghost_layer_depth
    depth = state.shape[1]
    joined = jnp.concatenate([state, kappa[None]], axis=0)
    first_plane = joined[:, :, :ghost_layer_depth]
    last_plane = lax.dynamic_slice_in_dim(
        joined, box_count * box_cells - ghost_layer_depth, ghost_layer_depth, 2
    )
    packet = jnp.stack([first_plane, last_plane]).reshape(2, 7, depth * ghost_layer_depth)
    framed = extended_2(packet, (("curve", 0),), 1, False)
    from_before = jnp.where(segment == 0, packet[0], framed[0]).reshape(7, depth, ghost_layer_depth)
    from_after = jnp.where(segment == segments - 1, packet[1], framed[3]).reshape(
        7, depth, ghost_layer_depth
    )
    z_edges = jnp.stack([joined[:, 0], joined[:, -1]])
    z_wrapped = extended_2(z_edges, (("near", 0),), 1, True)
    stacked = jnp.concatenate([z_wrapped[0][:, None], joined, z_wrapped[3][:, None]], axis=1)
    before_col = jnp.pad(from_before, ((0, 0), (1, 1), (0, 0)), mode="edge")
    after_col = jnp.pad(from_after, ((0, 0), (1, 1), (0, 0)), mode="edge")
    broad = jnp.concatenate([before_col, stacked, after_col], axis=2)
    broad = lax.dynamic_update_slice_in_dim(
        broad, after_col, ghost_layer_depth + box_count * box_cells, 2
    )
    return compute_rate(broad[:6], broad[6], ghost_layer_depth)


def advance(state, kappa, box_count, time_step, segment, segments):
    half = state + time_step * section_rate(state, kappa, box_count, segment, segments)
    return 0.5 * state + 0.5 * (
        half + time_step * section_rate(half, kappa, box_count, segment, segments)
    )


def regroup(block, incoming, leaving, arriving, box_cells):
    last_axis = block.ndim - 1
    stacked = jnp.concatenate(
        [block, incoming * arriving.astype(block.dtype), jnp.zeros_like(incoming)], axis=last_axis
    )
    return lax.dynamic_slice_in_dim(
        stacked, leaving * box_cells, block.shape[last_axis] + box_cells, last_axis
    )


def local(primitive, conductivity, new_owner):
    segment = lax.axis_index("curve")
    segments = lax.axis_size("curve")
    box_cells = BW * BW
    held_boxes = primitive.shape[2] // box_cells
    top_speed = jnp.max(wave_bound(primitive))
    top_kappa = jnp.max(conductivity)
    top_speed, top_kappa = lax.pmax((top_speed, top_kappa), ("curve", "near"))
    time_step = COURANT / (top_speed + 6.0 * top_kappa)
    leaving = (new_owner[0] != segment).astype(jnp.int32)
    cell_slot = jnp.arange((held_boxes + 1) * box_cells) // box_cells
    arrived = shifted(
        (primitive[:, :, :box_cells], conductivity[:, :box_cells], new_owner[0:1]), "curve", -1
    )
    arriving = ((arrived[2][0] == segment) & (segment < segments - 1)).astype(jnp.int32)
    box_count = held_boxes - leaving + arriving
    valid = cell_slot < box_count
    filler = jnp.array([1.0, 0.0, 0.0, 0.0, 1.0, 0.0], jnp.float32)[:, None, None]
    prim_new = jnp.where(
        valid[None, None, :], regroup(primitive, arrived[0], leaving, arriving, box_cells), filler
    )
    kappa_new = jnp.where(
        valid[None, :], regroup(conductivity, arrived[1], leaving, arriving, box_cells), 0.1
    )
    final = advance(to_conserved(prim_new), kappa_new, box_count, time_step, segment, segments)
    result = jnp.where(valid[None, None, :], final, 0.0)
    return result[None]


def solution(mesh):
    in_specs = (P(None, "near", "curve"), P("near", "curve"), P("curve"))
    out_specs = P("curve", None, "near", None)
    return jax.shard_map(local, mesh=mesh, in_specs=in_specs, out_specs=out_specs, check_vma=False)
```

profile of v0, /device:TPU:64, one launch (start us, length us, event | category | flops | bytes accessed | tf_op | source)
XLA Modules:
  0.0 180.5 jit_solution(3078507955319214404)
XLA Ops:
  0.0 0.9 slice.998
  0.9 4.5 %collective-permute-start.1 = (f32[6,4,1024]{2,1,0:T(4,128)S(1)}, f32[6,4,1024]{2,1,0:T(4,128)S(1)}, u32[]{:S(2)}, u32[]{:S(2)}) collective-permute-start(f32[6,4,1024]{2,1,0:T(4,128)S(1)} %slice.998), channel_id=1, source_target_pairs={{8,0},{16,8},{24,16},{32,24},{40,32},{48,40},{56,48},{64,56},{72,6... | collective-permute-start | bytes 294920 | tf_op jit(solution)/shard_map/ppermute | solution.py:29
  5.4 3.3 %collective-permute-start = (s32[1]{0:T(128)S(1)}, s32[1]{0:T(128)}, u32[]{:S(2)}, u32[]{:S(2)}) collective-permute-start(s32[1]{0:T(128)S(1)} %bitcast.145), channel_id=1, source_target_pairs={{8,0},{16,8},{24,16},{32,24},{40,32},{48,40},{56,48},{64,56},{72,6... | collective-permute-start | bytes 20 | tf_op jit(solution)/shard_map/ppermute | solution.py:29
  8.7 3.3 %collective-permute-start.2 = (f32[4,1024]{1,0:T(4,128)S(1)}, f32[4,1024]{1,0:T(4,128)S(1)}, u32[]{:S(2)}, u32[]{:S(2)}) collective-permute-start(f32[4,1024]{1,0:T(4,128)S(1)} %slice.1008), channel_id=1, source_target_pairs={{8,0},{16,8},{24,16},{32,24},{40,32},{48,40},{56,48},{64,56},{72,6... | collective-permute-start | bytes 49160 | tf_op jit(solution)/shard_map/ppermute | solution.py:29
  12.0 1.6 add_reduce_fusion
  13.7 0.6 reduce_max.19
  14.3 115.8 %all-reduce = (f32[]{:T(128)}, f32[]{:T(128)}) all-reduce(f32[]{:T(128)} %add_reduce_fusion, f32[]{:T(128)} %reduce_max.19), channel_id=1, replica_groups=mesh['curve'=96,'near'=8] {'curve','near'}, use_global_device_ids=true, to_apply=%region_2.0 | all-reduce | flops 2 | bytes 16 | tf_op jit(solution)/shard_map/pmax | solution.py:202
  132.3 0.6 copy-done.2
  133.6 2.1 %collective-permute-start.6 = (f32[1,7,128]{2,1,0:T(8,128)S(1)}, f32[1,7,128]{2,1,0:T(8,128)S(1)}, u32[]{:S(2)}, u32[]{:S(2)}) collective-permute-start(f32[1,7,128]{2,1,0:T(8,128)S(1)} %slice.1015), channel_id=1, source_target_pairs={{8,0},{16,8},{24,16},{32,24},{40,32},{48,40},{56,48},{64,56},{72,6... | collective-permute-start | bytes 10760 | tf_op jit(solution)/shard_map/ppermute | solution.py:21
  135.8 0.8 collective-permute-start.5
  136.6 2.5 %collective-permute-done.6 = f32[1,7,128]{2,1,0:T(8,128)S(1)} collective-permute-done((f32[1,7,128]{2,1,0:T(8,128)S(1)}, f32[1,7,128]{2,1,0:T(8,128)S(1)}, u32[]{:S(2)}, u32[]{:S(2)}) %collective-permute-start.6) | collective-permute-done | bytes 3616 | tf_op jit(solution)/shard_map/ppermute | solution.py:21
  139.3 1.9 %collective-permute-start.3 = (f32[1,7,128]{2,1,0:T(8,128)S(1)}, f32[1,7,128]{2,1,0:T(8,128)S(1)}, u32[]{:S(2)}, u32[]{:S(2)}) collective-permute-start(f32[1,7,128]{2,1,0:T(8,128)S(1)} %slice.1010), channel_id=1, source_target_pairs={{0,8},{8,16},{16,24},{24,32},{32,40},{40,48},{48,56},{56,64},{64,7... | collective-permute-start | bytes 10760 | tf_op jit(solution)/shard_map/ppermute | solution.py:20
  141.3 5.6 %collective-permute-done.3 = f32[1,7,128]{2,1,0:T(8,128)S(1)} collective-permute-done((f32[1,7,128]{2,1,0:T(8,128)S(1)}, f32[1,7,128]{2,1,0:T(8,128)S(1)}, u32[]{:S(2)}, u32[]{:S(2)}) %collective-permute-start.3) | collective-permute-done | bytes 3616 | tf_op jit(solution)/shard_map/ppermute | solution.py:20
  147.1 0.3 pad_maximum_fusion
  147.4 0.5 concatenate.162
  147.9 1.2 dynamic_update_slice.6
  152.5 0.9 fusion.26
  154.1 0.9 fusion.4
  155.3 0.5 fusion.10
  156.0 0.6 fusion.32
  156.7 2.0 %collective-permute-start.10 = (f32[1,7,128]{2,1,0:T(8,128)S(1)}, f32[1,7,128]{2,1,0:T(8,128)S(1)}, u32[]{:S(2)}, u32[]{:S(2)}) collective-permute-start(f32[1,7,128]{2,1,0:T(8,128)S(1)} %slice.1096), channel_id=1, source_target_pairs={{8,0},{16,8},{24,16},{32,24},{40,32},{48,40},{56,48},{64,56},{72,6... | collective-permute-start | bytes 10760 | tf_op jit(solution)/shard_map/ppermute | solution.py:21
  159.0 0.5 collective-permute-start.8
  159.5 2.7 %collective-permute-done.10 = f32[1,7,128]{2,1,0:T(8,128)S(1)} collective-permute-done((f32[1,7,128]{2,1,0:T(8,128)S(1)}, f32[1,7,128]{2,1,0:T(8,128)S(1)}, u32[]{:S(2)}, u32[]{:S(2)}) %collective-permute-start.10) | collective-permute-done | bytes 3616 | tf_op jit(solution)/shard_map/ppermute | solution.py:21
  162.4 2.1 %collective-permute-start.7 = (f32[1,7,128]{2,1,0:T(8,128)S(1)}, f32[1,7,128]{2,1,0:T(8,128)S(1)}, u32[]{:S(2)}, u32[]{:S(2)}) collective-permute-start(f32[1,7,128]{2,1,0:T(8,128)S(1)} %slice.1091), channel_id=1, source_target_pairs={{0,8},{8,16},{16,24},{24,32},{32,40},{40,48},{48,56},{56,64},{64,7... | collective-permute-start | bytes 10760 | tf_op jit(solution)/shard_map/ppermute | solution.py:20
  164.6 5.5 %collective-permute-done.7 = f32[1,7,128]{2,1,0:T(8,128)S(1)} collective-permute-done((f32[1,7,128]{2,1,0:T(8,128)S(1)}, f32[1,7,128]{2,1,0:T(8,128)S(1)}, u32[]{:S(2)}, u32[]{:S(2)}) %collective-permute-start.7) | collective-permute-done | bytes 3616 | tf_op jit(solution)/shard_map/ppermute | solution.py:20
  170.2 0.3 pad_maximum_fusion.1
  170.5 0.5 concatenate.179
  171.0 1.2 dynamic_update_slice.7
  175.6 0.9 fusion.16
  177.3 0.9 fusion.1
  178.5 0.5 fusion.7
  179.2 1.4 select_bitcast_fusion
  (131 shorter events, 10.8 us)
Async XLA Ops:
  0.0 8.7 %copy-start.1 = (f32[4,3072]{1,0:T(4,128)S(1)}, f32[4,3072]{1,0:T(4,128)}, u32[]{:S(2)}) copy-start(f32[4,3072]{1,0:T(4,128)} %param.41) | copy-start | bytes 147460
  0.9 4.5 %copy-start.3 = (s32[3]{0:T(128)S(1)}, s32[3]{0:T(128)}, u32[]{:S(2)}) copy-start(s32[3]{0:T(128)} %param.42) | copy-start | bytes 40
  0.9 131.3 %collective-permute-start.1 = (f32[6,4,1024]{2,1,0:T(4,128)S(1)}, f32[6,4,1024]{2,1,0:T(4,128)S(1)}, u32[]{:S(2)}, u32[]{:S(2)}) collective-permute-start(f32[6,4,1024]{2,1,0:T(4,128)S(1)} %slice.998), channel_id=1, source_target_pairs={{8,0},{16,8},{24,16},{32,24},{40,32},{48,40},{56,48},{64,56},{72,6... | collective-permute-start | bytes 294920 | tf_op jit(solution)/shard_map/ppermute | solution.py:29
  5.4 126.1 %collective-permute-start = (s32[1]{0:T(128)S(1)}, s32[1]{0:T(128)}, u32[]{:S(2)}, u32[]{:S(2)}) collective-permute-start(s32[1]{0:T(128)S(1)} %bitcast.145), channel_id=1, source_target_pairs={{8,0},{16,8},{24,16},{32,24},{40,32},{48,40},{56,48},{64,56},{72,6... | collective-permute-start | bytes 20 | tf_op jit(solution)/shard_map/ppermute | solution.py:29
  8.7 123.5 %collective-permute-start.2 = (f32[4,1024]{1,0:T(4,128)S(1)}, f32[4,1024]{1,0:T(4,128)S(1)}, u32[]{:S(2)}, u32[]{:S(2)}) collective-permute-start(f32[4,1024]{1,0:T(4,128)S(1)} %slice.1008), channel_id=1, source_target_pairs={{8,0},{16,8},{24,16},{32,24},{40,32},{48,40},{56,48},{64,56},{72,6... | collective-permute-start | bytes 49160 | tf_op jit(solution)/shard_map/ppermute | solution.py:29
  12.0 120.3 %copy-start = (f32[6,4,3072]{2,1,0:T(4,128)S(1)}, f32[6,4,3072]{2,1,0:T(4,128)}, u32[]{:S(2)}) copy-start(f32[6,4,3072]{2,1,0:T(4,128)} %param.40) | copy-start | bytes 884740
  132.3 0.7 copy-start.2
  133.6 5.5 %collective-permute-start.6 = (f32[1,7,128]{2,1,0:T(8,128)S(1)}, f32[1,7,128]{2,1,0:T(8,128)S(1)}, u32[]{:S(2)}, u32[]{:S(2)}) collective-permute-start(f32[1,7,128]{2,1,0:T(8,128)S(1)} %slice.1015), channel_id=1, source_target_pairs={{8,0},{16,8},{24,16},{32,24},{40,32},{48,40},{56,48},{64,56},{72,6... | collective-permute-start | bytes 10760 | tf_op jit(solution)/shard_map/ppermute | solution.py:21
  135.8 11.2 %collective-permute-start.5 = (f32[1,7,4096]{2,0,1:T(1,128)S(1)}, f32[1,7,4096]{2,0,1:T(1,128)S(1)}, u32[]{:S(2)}, u32[]{:S(2)}) collective-permute-start(f32[1,7,4096]{2,0,1:T(1,128)S(1)} %get-tuple-element.270), channel_id=1, source_target_pairs={{1,0},{2,1},{3,2},{4,3},{5,4},{6,5},{7,6},{0,7},{9,8},{10,9},{11,1... | collective-permute-start | bytes 344072 | tf_op jit(solution)/shard_map/ppermute | solution.py:21
  136.6 10.4 %collective-permute-start.4 = (f32[1,7,4096]{2,0,1:T(1,128)S(1)}, f32[1,7,4096]{2,0,1:T(1,128)S(1)}, u32[]{:S(2)}, u32[]{:S(2)}) collective-permute-start(f32[1,7,4096]{2,0,1:T(1,128)S(1)} %get-tuple-element.269), channel_id=1, source_target_pairs={{0,1},{1,2},{2,3},{3,4},{4,5},{5,6},{6,7},{7,0},{8,9},{9,10},{10,1... | collective-permute-start | bytes 344072 | tf_op jit(solution)/shard_map/ppermute | solution.py:20
  139.3 7.6 %collective-permute-start.3 = (f32[1,7,128]{2,1,0:T(8,128)S(1)}, f32[1,7,128]{2,1,0:T(8,128)S(1)}, u32[]{:S(2)}, u32[]{:S(2)}) collective-permute-start(f32[1,7,128]{2,1,0:T(8,128)S(1)} %slice.1010), channel_id=1, source_target_pairs={{0,8},{8,16},{16,24},{24,32},{32,40},{40,48},{48,56},{56,64},{64,7... | collective-permute-start | bytes 10760 | tf_op jit(solution)/shard_map/ppermute | solution.py:20
  156.7 5.5 %collective-permute-start.10 = (f32[1,7,128]{2,1,0:T(8,128)S(1)}, f32[1,7,128]{2,1,0:T(8,128)S(1)}, u32[]{:S(2)}, u32[]{:S(2)}) collective-permute-start(f32[1,7,128]{2,1,0:T(8,128)S(1)} %slice.1096), channel_id=1, source_target_pairs={{8,0},{16,8},{24,16},{32,24},{40,32},{48,40},{56,48},{64,56},{72,6... | collective-permute-start | bytes 10760 | tf_op jit(solution)/shard_map/ppermute | solution.py:21
  158.9 11.2 %collective-permute-start.9 = (f32[1,7,4096]{2,0,1:T(1,128)S(1)}, f32[1,7,4096]{2,0,1:T(1,128)S(1)}, u32[]{:S(2)}, u32[]{:S(2)}) collective-permute-start(f32[1,7,4096]{2,0,1:T(1,128)S(1)} %get-tuple-element.268), channel_id=1, source_target_pairs={{1,0},{2,1},{3,2},{4,3},{5,4},{6,5},{7,6},{0,7},{9,8},{10,9},{11,1... | collective-permute-start | bytes 344072 | tf_op jit(solution)/shard_map/ppermute | solution.py:21
  159.0 11.2 %collective-permute-start.8 = (f32[1,7,4096]{2,0,1:T(1,128)S(1)}, f32[1,7,4096]{2,0,1:T(1,128)S(1)}, u32[]{:S(2)}, u32[]{:S(2)}) collective-permute-start(f32[1,7,4096]{2,0,1:T(1,128)S(1)} %get-tuple-element.267), channel_id=1, source_target_pairs={{0,1},{1,2},{2,3},{3,4},{4,5},{5,6},{6,7},{7,0},{8,9},{9,10},{10,1... | collective-permute-start | bytes 344072 | tf_op jit(solution)/shard_map/ppermute | solution.py:20
  162.4 7.6 %collective-permute-start.7 = (f32[1,7,128]{2,1,0:T(8,128)S(1)}, f32[1,7,128]{2,1,0:T(8,128)S(1)}, u32[]{:S(2)}, u32[]{:S(2)}) collective-permute-start(f32[1,7,128]{2,1,0:T(8,128)S(1)} %slice.1091), channel_id=1, source_target_pairs={{0,8},{8,16},{16,24},{24,32},{32,40},{40,48},{48,56},{56,64},{64,7... | collective-permute-start | bytes 10760 | tf_op jit(solution)/shard_map/ppermute | solution.py:20
where the time goes:
time: 181 us
  blocking collectives  116 us (64%)
  starting transfers between devices  20.3 us (11%)
  waiting for transfers between devices  16.3 us (9%)
  other arithmetic  13.7 us (8%)
  local copies, waits for them, and re-layouts  11.6 us (6%)
  between operations  2.79 us (2%)
    pmax x1, blocking collectives, local(): top_speed, top_kappa = lax.pmax((top_speed, top_kappa), ('curve', 'near'))  116 us
    ppermute x4, waiting for transfers between devices, extended_2(): before = lax.ppermute(last, axis, up)  11.1 us
    ppermute x3, starting transfers between devices, shifted(): return lax.ppermute(block, axis, route)  11 us
    ppermute x4, waiting for transfers between devices, extended_2(): after = lax.ppermute(first, axis, down)  5.2 us
    ppermute x4, starting transfers between devices, extended_2(): after = lax.ppermute(first, axis, down)  4.85 us
    sub x6, other arithmetic, face_flux(): 0.5 * (lower_f + upper_f)  4.58 us
    ppermute x4, starting transfers between devices, extended_2(): before = lax.ppermute(last, axis, up)  4.51 us
  transfers between devices with their start and end apart: 11, of which 4 were waited for; matrix products, arithmetic and copies ran while one was open for 2% of the time, Pallas kernels for 0%

commit v1 on v0

v1 whole, which is shorter than its diff:
```python
import functools

import jax
import jax.numpy as jnp
from jax import lax
from jax.experimental import pallas as pl
from jax.experimental.pallas import tpu as pltpu
from jax.sharding import PartitionSpec as P

BW = 32
BOXES = 3
DEPTH = 4
LANES = 128
OWN = 24
ROWS = 40
NEXT = 40
PREV = 8
Y_CHIPS = 8
MESH = pl.DeviceIdType.MESH
F32 = jnp.float32


def lane_of(shape):
    return lax.broadcasted_iota(jnp.int32, shape, len(shape) - 1)


def row_of(shape):
    return lax.broadcasted_iota(jnp.int32, shape, 0)


def upper_y(v, ypos):
    return jnp.where(ypos == BW - 1, pltpu.roll(v, BW - 1, 1), pltpu.roll(v, LANES - 1, 1))


def lower_y(v, ypos):
    return jnp.where(ypos == 0, pltpu.roll(v, LANES - BW + 1, 1), pltpu.roll(v, 1, 1))


def upper_x(v, lane):
    above = pltpu.roll(v, v.shape[0] - 1, 0)
    return pltpu.roll(jnp.where(lane < BW, above, v), LANES - BW, 1)


def lower_x(v, lane):
    below = pltpu.roll(v, 1, 0)
    return pltpu.roll(jnp.where(lane >= LANES - BW, below, v), BW, 1)


def derive(cons):
    r, mx, my, mz, energy = cons[:5]
    inv = 1.0 / r
    vx, vy, vz = mx * inv, my * inv, mz * inv
    pressure = 0.4 * (energy - 0.5 * (mx * vx + my * vy + mz * vz))
    temp = pressure * inv
    return 0.5 * vx, 0.5 * vy, 0.5 * vz, 0.5 * jnp.sqrt(1.4 * temp), 0.5 * pressure, temp


def face(lo, hi, k):
    lu, ld, lc = lo
    hu, hd, hc = hi
    lw, hw = ld[k], hd[k]
    top = jnp.maximum(jnp.abs(lw) + ld[3], jnp.abs(hw) + hd[3])
    lf, hf = lw + top, hw - top
    flux = [a * lf + b * hf for a, b in zip(lu, hu)]
    flux[1 + k] = flux[1 + k] + (ld[4] + hd[4])
    work = ld[4] * lw + hd[4] * hw
    flux[4] = flux[4] + (work + work) - (lc + hc) * (hd[5] - ld[5])
    return flux


def mapped(cell, fn):
    u, d, c = cell
    return [fn(a) for a in u], [fn(a) for a in d], fn(c)


def plane_rate(get, z):
    mid = get(z)
    shape = mid[2].shape
    lane = lane_of(shape)
    ypos = lane % BW
    flux = face(mid, mapped(mid, lambda v: upper_x(v, lane)), 0)
    total = [lower_x(f, lane) - f for f in flux]
    flux = face(mid, mapped(mid, lambda v: upper_y(v, ypos)), 1)
    total = [t + (lower_y(f, ypos) - f) for t, f in zip(total, flux)]
    flux = face(mid, get(z + 1), 2)
    total = [t - f for t, f in zip(total, flux)]
    flux = face(get(z - 1), mid, 2)
    return [t + f for t, f in zip(total, flux)]


def spread(ref, f, row):
    return jnp.broadcast_to(ref[f, row : row + 1], (8, LANES))


def conserved(prim):
    r, vx, vy, vz, p, s = prim
    energy = p * 2.5 + 0.5 * r * (vx * vx + vy * vy + vz * vz)
    return r, r * vx, r * vy, r * vz, energy, r * s


def exchange_kernel(
    n_curve, n_near,
    prim_hbm, cond_hbm, owner_hbm,
    u_out, rate_out, top_out, flag_out,
    raw, from_next, from_prev, ext, der, low_planes, high_planes,
    sent, got_near, got_y, got_z, flag_sent, flag_got, owner,
    load_sem, near_send, near_recv, y_send, y_recv, z_send, z_recv, halo_send, halo_recv,
):
    n_y = Y_CHIPS
    n_z = n_curve // n_y
    curve, near = lax.axis_index("curve"), lax.axis_index("near")
    at_y, at_z = curve % n_y, curve // n_y
    loads = [
        pltpu.make_async_copy(prim_hbm, raw.at[pl.ds(0, 6)], load_sem.at[0]),
        pltpu.make_async_copy(cond_hbm, raw.at[6], load_sem.at[1]),
        pltpu.make_async_copy(owner_hbm, owner, load_sem.at[2]),
    ]
    for copy in loads:
        copy.start()

    def far_first(n):
        return sorted(range(1, n), key=lambda j: -min(j, n - j))

    def near_at(j):
        return (curve, (near + j) % n_near)

    def y_at(j):
        return (at_z * n_y + (at_y + j) % n_y, near)

    def z_at(j):
        return (((at_z + j) % n_z) * n_y + at_y, near)

    before, after = ((curve + n_curve - 1) % n_curve, near), ((curve + 1) % n_curve, near)
    partners = [near_at(j) for j in far_first(n_near)] + [y_at(j) for j in far_first(n_y)]
    partners += [z_at(j) for j in far_first(n_z)] + [before, after]
    barrier = pltpu.get_barrier_semaphore()
    for device in partners:
        pl.semaphore_signal(barrier, inc=1, device_id=device, device_id_type=MESH)

    for copy in loads:
        copy.wait()
    speed, cond = None, None
    for i in range(0, raw.shape[1], 8):
        r, vx, vy, vz, p = (raw[f, i : i + 8] for f in range(5))
        here = jnp.abs(vx) + jnp.abs(vy) + jnp.abs(vz) + 3.0 * jnp.sqrt(1.4 * p / r)
        k = raw[6, i : i + 8]
        speed = here if speed is None else jnp.maximum(speed, here)
        cond = k if cond is None else jnp.maximum(cond, k)
    lane8 = lane_of((8, LANES))
    both = jnp.where(
        lane8 < LANES // 2,
        jnp.maximum(speed, pltpu.roll(speed, LANES // 2, 1)),
        jnp.maximum(cond, pltpu.roll(cond, LANES // 2, 1)),
    )
    best = jnp.max(both, axis=0, keepdims=True)
    sent[0] = best
    leaving = jnp.where(owner[0] != curve, 1.0, 0.0).astype(F32)
    flag_sent[...] = jnp.full(flag_sent.shape, leaving, F32)

    pl.semaphore_wait(barrier, len(partners))

    def exchange(stage, got, at, n, send_sem, recv_sem):
        copies = {}
        for j in far_first(n):
            copies[j] = pltpu.make_async_remote_copy(
                src_ref=sent.at[stage], dst_ref=got.at[j - 1], send_sem=send_sem.at[j - 1],
                recv_sem=recv_sem.at[j - 1], device_id=at(j), device_id_type=MESH,
            )
            copies[j].start()
        return [copies[j] for j in range(1, n)]

    def gathered(copies, got, value):
        for copy in copies:
            copy.wait_recv()
        rows = [value] + [got[i] for i in range(len(copies))]
        while len(rows) > 1:
            rows = [jnp.maximum(*rows[i : i + 2]) if i + 1 < len(rows) else rows[i] for i in range(0, len(rows), 2)]
        return rows[0]

    def halo(i, src, dst, device):
        copy = pltpu.make_async_remote_copy(
            src_ref=src, dst_ref=dst, send_sem=halo_send.at[i], recv_sem=halo_recv.at[i],
            device_id=device, device_id_type=MESH,
        )
        copy.start()
        return copy

    near_copies = exchange(0, got_near, near_at, n_near, near_send, near_recv)
    curve_copies = [
        halo(0, raw.at[:, pl.ds(0, NEXT)], from_next, before),
        halo(1, raw.at[:, pl.ds(raw.shape[1] - PREV, PREV)], from_prev, after),
        halo(2, flag_sent, flag_got, before),
    ]

    for z in range(DEPTH):
        for i in range(OWN // 8):
            rows = pl.ds(i * 8 * DEPTH + z, 8, stride=DEPTH)
            for f, value in enumerate(conserved([raw[f, rows] for f in range(6)])):
                ext[f, 2 + z, i * 8 : i * 8 + 8] = value
            ext[6, 2 + z, i * 8 : i * 8 + 8] = 0.5 * raw[6, rows]

    best = gathered(near_copies, got_near, best)
    sent[1] = best
    y_copies = exchange(1, got_y, y_at, n_y, y_send, y_recv)

    first, last = curve == 0, curve == n_curve - 1
    row8 = row_of((8, LANES))
    for copy in curve_copies:
        copy.wait_recv()
    for z in range(DEPTH):
        fourth, sides = [], []
        for f in range(7):
            v = from_next[f, pl.ds(z, 8, stride=DEPTH)]
            edge = pltpu.roll(spread(raw, f, (OWN - 1) * DEPTH + z), BW, 1)
            fourth.append(jnp.where(jnp.logical_and(last, row8 == 0), edge, v))
            after_row = spread(from_next, f, 8 * DEPTH + z)
            before_row = spread(from_prev, f, PREV - DEPTH + z)
            edge = pltpu.roll(spread(raw, f, z), LANES - BW, 1)
            before_row = jnp.where(first, edge, before_row)
            sides.append(jnp.where(row8 == 7, before_row, after_row))
        for i, group in ((OWN // 8, fourth), (OWN // 8 + 1, sides)):
            for f, value in enumerate(conserved(group[:6])):
                ext[f, 2 + z, i * 8 : i * 8 + 8] = value
            ext[6, 2 + z, i * 8 : i * 8 + 8] = 0.5 * group[6]

    plane_copies = [
        halo(3, ext.at[:, pl.ds(4, 2)], low_planes, near_at(1)),
        halo(4, ext.at[:, pl.ds(2, 2)], high_planes, near_at(n_near - 1)),
    ]

    def fill_derived(z):
        for i, value in enumerate(derive([ext[f, z] for f in range(5)])):
            der[i, z] = value

    def cell(z):
        return [ext[f, z] for f in range(6)], [der[i, z] for i in range(6)], ext[6, z]

    def fill_rate(z):
        for f, value in enumerate(plane_rate(cell, z)):
            rate_out[f, z - 1] = value

    lax.fori_loop(2, 6, lambda z, c: (fill_derived(z), c)[1], 0)

    best = gathered(y_copies, got_y, best)
    sent[2] = best
    z_copies = exchange(2, got_z, z_at, n_z, z_send, z_recv)

    lax.fori_loop(3, 5, lambda z, c: (fill_rate(z), c)[1], 0)

    for copy in plane_copies:
        copy.wait()
    for i in range(2):
        for f in range(7):
            ext[f, i] = low_planes[f, i]
            ext[f, 6 + i] = high_planes[f, i]
    for z in (0, 1, 6, 7):
        fill_derived(z)
    lax.fori_loop(0, 2, lambda i, c: (fill_rate(1 + 4 * i), c)[1], 0)
    lax.fori_loop(0, 2, lambda i, c: (fill_rate(2 + 4 * i), c)[1], 0)
    for f in range(7):
        for z in range(6):
            u_out[f, z] = ext[f, z + 1]
    flag_out[0:1] = flag_sent[...]
    flag_out[1:2] = flag_got[...]

    top_out[...] = gathered(z_copies, got_z, best)
    for copy in near_copies + curve_copies + y_copies + z_copies:
        copy.wait_send()


def finish_kernel(n_curve, u_ref, rate_ref, top_ref, flag_ref, out_ref, half, der):
    curve = lax.axis_index("curve")
    first, last = curve == 0, curve == n_curve - 1
    top = top_ref[...]
    lane = lane_of(top.shape)
    speed = jnp.max(jnp.where(lane < LANES // 2, top, 0.0), axis=1, keepdims=True)
    cond = jnp.max(jnp.where(lane < LANES // 2, 0.0, top), axis=1, keepdims=True)
    step = 0.8 / (speed + 6.0 * cond)
    row = row_of((ROWS, LANES))

    def fill_half(z, carry):
        values = []
        for f in range(6):
            v = u_ref[f, z] + step * rate_ref[f, z]
            left = pltpu.roll(jnp.broadcast_to(v[0:1], v.shape), LANES - BW, 1)
            right = pltpu.roll(jnp.broadcast_to(v[OWN - 1 : OWN], v.shape), BW, 1)
            v = jnp.where(jnp.logical_and(first, row == ROWS - 1), left, v)
            v = jnp.where(jnp.logical_and(last, row == OWN), right, v)
            half[f, z] = v
            values.append(v)
        for i, value in enumerate(derive(values[:5])):
            der[i, z] = value
        return carry

    lax.fori_loop(0, 6, fill_half, 0)
    leaving = flag_ref[0:1] > 0.5
    arriving = flag_ref[1:2] > 0.5

    def cell(z):
        return [half[f, z] for f in range(6)], [der[i, z] for i in range(6)], u_ref[6, z]

    def fill_out(z, carry):
        rates = plane_rate(cell, z)
        for f in range(6):
            final = 0.5 * u_ref[f, z] + 0.5 * (half[f, z] + step * rates[f])
            box = [final[8 * j : 8 * j + 8] for j in range(BOXES + 1)]
            slot = [jnp.where(leaving, box[j + 1], box[j]) for j in range(BOXES)]
            slot[2] = jnp.where(jnp.logical_and(leaving, jnp.logical_not(arriving)), 0.0, slot[2])
            slot.append(jnp.where(jnp.logical_and(arriving, jnp.logical_not(leaving)), box[3], 0.0))
            for j, value in enumerate(slot):
                out_ref[f, pl.ds(j * 8 * DEPTH + z - 1, 8, stride=DEPTH)] = value
        return carry

    lax.fori_loop(1, 5, fill_out, 0)


def local(n_curve, n_near, primitive, conductivity, new_owner):
    rows = OWN * DEPTH
    prim = primitive.reshape(6, DEPTH, OWN, LANES).transpose(0, 2, 1, 3).reshape(6, rows, LANES)
    cond = conductivity.reshape(DEPTH, OWN, LANES).transpose(1, 0, 2).reshape(rows, LANES)
    n_y, n_z = Y_CHIPS, n_curve // Y_CHIPS
    anywhere = pl.BlockSpec(memory_space=pl.ANY)
    vmem = pl.BlockSpec(memory_space=pltpu.VMEM)
    dma = pltpu.SemaphoreType.DMA
    state = pl.pallas_call(
        functools.partial(exchange_kernel, n_curve, n_near),
        out_shape=(
            pltpu.VMEM((7, 6, ROWS, LANES), F32),
            pltpu.VMEM((6, 6, ROWS, LANES), F32),
            pltpu.VMEM((1, LANES), F32),
            pltpu.VMEM((2, LANES), F32),
        ),
        in_specs=[anywhere] * 3,
        out_specs=(vmem,) * 4,
        scratch_shapes=[
            pltpu.VMEM((7, rows, LANES), F32),
            pltpu.VMEM((7, NEXT, LANES), F32),
            pltpu.VMEM((7, PREV, LANES), F32),
            pltpu.VMEM((7, 8, ROWS, LANES), F32),
            pltpu.VMEM((6, 8, ROWS, LANES), F32),
            pltpu.VMEM((7, 2, ROWS, LANES), F32),
            pltpu.VMEM((7, 2, ROWS, LANES), F32),
            pltpu.VMEM((3, 1, LANES), F32),
            pltpu.VMEM((n_near - 1, 1, LANES), F32),
            pltpu.VMEM((n_y - 1, 1, LANES), F32),
            pltpu.VMEM((n_z - 1, 1, LANES), F32),
            pltpu.VMEM((1, LANES), F32),
            pltpu.VMEM((1, LANES), F32),
            pltpu.SMEM((BOXES,), jnp.int32),
            dma((3,)),
            dma((n_near - 1,)), dma((n_near - 1,)),
            dma((n_y - 1,)), dma((n_y - 1,)),
            dma((n_z - 1,)), dma((n_z - 1,)),
            dma((5,)), dma((5,)),
        ],
        compiler_params=pltpu.CompilerParams(collective_id=0, has_side_effects=True),
        name="exchange",
    )(prim, cond, new_owner)
    out = pl.pallas_call(
        functools.partial(finish_kernel, n_curve),
        out_shape=jax.ShapeDtypeStruct((6, 32 * DEPTH, LANES), F32),
        in_specs=[vmem] * 4,
        out_specs=vmem,
        scratch_shapes=[pltpu.VMEM((6, 6, ROWS, LANES), F32)] * 2,
        name="finish",
    )(*(pltpu.with_memory_space_constraint(v, pltpu.VMEM) for v in state))
    out = out.reshape(6, 32, DEPTH, LANES).transpose(0, 2, 1, 3).reshape(6, DEPTH, 32 * LANES)
    return out[None]


def solution(mesh):
    n_curve, n_near = mesh.shape["curve"], mesh.shape["near"]
    return jax.shard_map(
        functools.partial(local, n_curve, n_near),
        mesh=mesh,
        in_specs=(P(None, "near", "curve"), P("near", "curve"), P("curve")),
        out_specs=P("curve", None, "near", None),
        check_vma=False,
    )
```

time: 181 us -> 36.4 us (0.20)
  the two profiles are of different devices: /device:TPU:64 before, /device:TPU:1 now
where the time goes in v1:
time: 36.4 us; the launch traced here: 36.2 us
  Pallas kernels  36.2 us (99%)
    pallas_call x1, Pallas kernels, local(): pl.pallas_call(functools.partial(exchange_kernel, n_curve, n_near), out_s...  33 us
    pallas_call x1, Pallas kernels, local(): pl.pallas_call(functools.partial(finish_kernel, n_curve), out_shape=jax.S...  3.2 us

profile of v1, /device:TPU:1, one launch (start us, length us, event | category | flops | bytes accessed | tf_op | source)
XLA Modules:
  0.0 36.2 jit_solution(2844020416931947350)
XLA Ops:
  0.0 33.0 %exchange.1 = (f32[7,6,40,128]{3,2,1,0:T(8,128)S(1)}, f32[6,6,40,128]{3,2,1,0:T(8,128)S(1)}, f32[1,128]{1,0:T(1,128)S(1)}, f32[2,128]{1,0:T(2,128)S(1)}) custom-call(f32[6,96,128]{2,1,0:T(8,128)} %bitcast.15, f32[96,128]{1,0:T(8,128)} %bitcast.16, s32[3]{0:T(128)} %owner_hbm.1), custom_call_target="tpu_custom_call" | custom-call | tf_op jit(solution)/shard_map/exchange/pallas_call | solution.py:325
  33.1 3.2 %finish.1 = f32[6,128,128]{2,1,0:T(8,128)} custom-call(f32[7,6,40,128]{3,2,1,0:T(8,128)S(1)} %get-tuple-element.9.u_ref, f32[6,6,40,128]{3,2,1,0:T(8,128)S(1)} %get-tuple-element.10.rate_ref, f32[1,128]{1,0:T(1,128)S(1)} %get-tuple-element.11.top_ref, f32[2,128]{1,0:T(2,128)S(1)} %get-tuple-element.12.flag_ref), custom_call_target="tpu_custom_call" | custom-call | tf_op jit(solution)/shard_map/finish/pallas_call | solution.py:359

commit v2 on v1

--- a/solution.py
+++ b/solution.py
@@ -16,6 +16,7 @@
 NEXT = 40
 PREV = 8
 Y_CHIPS = 8
+RELAY = 3
 MESH = pl.DeviceIdType.MESH
 F32 = jnp.float32
 
@@ -103,13 +104,14 @@
     prim_hbm, cond_hbm, owner_hbm,
     u_out, rate_out, top_out, flag_out,
     raw, from_next, from_prev, ext, der, low_planes, high_planes,
-    sent, got_near, got_y, got_z, flag_sent, flag_got, owner,
-    load_sem, near_send, near_recv, y_send, y_recv, z_send, z_recv, halo_send, halo_recv,
+    sent, got_plane, got_column, flag_sent, flag_got, owner,
+    load_sem, stage_send, stage_recv, halo_send, halo_recv, relay,
 ):
-    n_y = Y_CHIPS
+    n_y, n_x = Y_CHIPS, n_near // 2
     n_z = n_curve // n_y
     curve, near = lax.axis_index("curve"), lax.axis_index("near")
-    at_y, at_z = curve % n_y, curve // n_y
+    y, z_chip, x, core = lax.rem(curve, n_y), lax.div(curve, n_y), lax.div(near, 2), lax.rem(near, 2)
+    first, last = curve == 0, curve == n_curve - 1
     loads = [
         pltpu.make_async_copy(prim_hbm, raw.at[pl.ds(0, 6)], load_sem.at[0]),
         pltpu.make_async_copy(cond_hbm, raw.at[6], load_sem.at[1]),
@@ -118,24 +120,46 @@
     for copy in loads:
         copy.start()
 
-    def far_first(n):
-        return sorted(range(1, n), key=lambda j: -min(j, n - j))
-
-    def near_at(j):
-        return (curve, (near + j) % n_near)
-
-    def y_at(j):
-        return (at_z * n_y + (at_y + j) % n_y, near)
-
-    def z_at(j):
-        return (((at_z + j) % n_z) * n_y + at_y, near)
-
-    before, after = ((curve + n_curve - 1) % n_curve, near), ((curve + 1) % n_curve, near)
-    partners = [near_at(j) for j in far_first(n_near)] + [y_at(j) for j in far_first(n_y)]
-    partners += [z_at(j) for j in far_first(n_z)] + [before, after]
+    def ring(j, n):
+        return min(j % n, -j % n)
+
+    ys = [lax.rem(y + j, n_y) for j in range(n_y)]
+    xs = [2 * lax.rem(x + j, n_x) for j in range(n_x)]
+    zs = [n_y * lax.rem(z_chip + j, n_z) for j in range(n_z)]
+
+    def plane_at(offset, side):
+        return (zs[0] + ys[offset[1]], xs[offset[0]] + side)
+
+    def column_at(j, side):
+        return (zs[j] + ys[0], xs[0] + side)
+
+    plane = sorted(
+        ((i, j) for i in range(n_x) for j in range(n_y)),
+        key=lambda o: -ring(o[0], n_x) - ring(o[1], n_y),
+    )
+    slot_of = {o: o[0] * n_y + o[1] for o in plane}
+    others = [o for o in plane if slot_of[o] > 0]
+    n_plane = len(plane)
+    column = sorted(range(n_z), key=lambda j: -ring(j, n_z))
+    close = [j for j in column if 0 < ring(j, n_z) <= RELAY]
+    relays = [RELAY, n_z - RELAY] if n_z // 2 > RELAY else []
+    before, after = (lax.rem(curve + n_curve - 1, n_curve), near), (lax.rem(curve + 1, n_curve), near)
     barrier = pltpu.get_barrier_semaphore()
-    for device in partners:
-        pl.semaphore_signal(barrier, inc=1, device_id=device, device_id_type=MESH)
+
+    def greet(devices):
+        for device in devices:
+            pl.semaphore_signal(barrier, inc=1, device_id=device, device_id_type=MESH)
+
+    @pl.when(core == 0)
+    def _():
+        greet([plane_at(o, 1) for o in plane] + [column_at(j, 1) for j in close])
+
+    @pl.when(core == 1)
+    def _():
+        greet([plane_at(o, 1) for o in others] + [plane_at(o, 0) for o in plane])
+        greet([column_at(j, 1) for j in close])
+
+    greet([before, after])
 
     for copy in loads:
         copy.wait()
@@ -157,40 +181,53 @@
     leaving = jnp.where(owner[0] != curve, 1.0, 0.0).astype(F32)
     flag_sent[...] = jnp.full(flag_sent.shape, leaving, F32)
 
-    pl.semaphore_wait(barrier, len(partners))
-
-    def exchange(stage, got, at, n, send_sem, recv_sem):
-        copies = {}
-        for j in far_first(n):
-            copies[j] = pltpu.make_async_remote_copy(
-                src_ref=sent.at[stage], dst_ref=got.at[j - 1], send_sem=send_sem.at[j - 1],
-                recv_sem=recv_sem.at[j - 1], device_id=at(j), device_id_type=MESH,
-            )
-            copies[j].start()
-        return [copies[j] for j in range(1, n)]
-
-    def gathered(copies, got, value):
-        for copy in copies:
-            copy.wait_recv()
-        rows = [value] + [got[i] for i in range(len(copies))]
+    def send(stage, got, slot, device):
+        pltpu.make_async_remote_copy(
+            src_ref=sent.at[stage], dst_ref=got.at[slot], send_sem=stage_send.at[stage],
+            recv_sem=stage_recv.at[stage], device_id=device, device_id_type=MESH,
+        ).start()
+
+    def wait_rows(sem, got, count):
+        rows = got.at[pl.ds(0, count)]
+        pltpu.make_async_copy(rows, rows, sem).wait()
+
+    def largest(rows):
         while len(rows) > 1:
             rows = [jnp.maximum(*rows[i : i + 2]) if i + 1 < len(rows) else rows[i] for i in range(0, len(rows), 2)]
         return rows[0]
 
     def halo(i, src, dst, device):
-        copy = pltpu.make_async_remote_copy(
+        return pltpu.make_async_remote_copy(
             src_ref=src, dst_ref=dst, send_sem=halo_send.at[i], recv_sem=halo_recv.at[i],
             device_id=device, device_id_type=MESH,
         )
-        copy.start()
-        return copy
-
-    near_copies = exchange(0, got_near, near_at, n_near, near_send, near_recv)
-    curve_copies = [
-        halo(0, raw.at[:, pl.ds(0, NEXT)], from_next, before),
-        halo(1, raw.at[:, pl.ds(raw.shape[1] - PREV, PREV)], from_prev, after),
-        halo(2, flag_sent, flag_got, before),
-    ]
+
+    @pl.when(core == 0)
+    def _():
+        pl.semaphore_wait(barrier, n_plane + 2)
+        for o in plane:
+            send(0, got_plane, n_plane - 1 + slot_of[o], plane_at(o, 1))
+
+    @pl.when(core == 1)
+    def _():
+        pl.semaphore_wait(barrier, 2 * n_plane - 1 + 2 * len(close) + 2)
+        for j in relays:
+            pl.semaphore_signal(relay, inc=1, device_id=column_at(j, 1), device_id_type=MESH)
+        for o in others:
+            send(0, got_plane, slot_of[o] - 1, plane_at(o, 1))
+
+    to_before = [halo(0, raw.at[:, pl.ds(0, NEXT)], from_next, before), halo(2, flag_sent, flag_got, before)]
+    to_after = [halo(1, raw.at[:, pl.ds(raw.shape[1] - PREV, PREV)], from_prev, after)]
+
+    @pl.when(jnp.logical_not(first))
+    def _():
+        for copy in to_before:
+            copy.start()
+
+    @pl.when(jnp.logical_not(last))
+    def _():
+        for copy in to_after:
+            copy.start()
 
     for z in range(DEPTH):
         for i in range(OWN // 8):
@@ -199,14 +236,30 @@
                 ext[f, 2 + z, i * 8 : i * 8 + 8] = value
             ext[6, 2 + z, i * 8 : i * 8 + 8] = 0.5 * raw[6, rows]
 
-    best = gathered(near_copies, got_near, best)
-    sent[1] = best
-    y_copies = exchange(1, got_y, y_at, n_y, y_send, y_recv)
-
-    first, last = curve == 0, curve == n_curve - 1
+    @pl.when(core == 1)
+    def _():
+        count = 2 * n_plane - 1
+        wait_rows(stage_recv.at[0], got_plane, count)
+        sent[1] = largest([sent[0]] + [got_plane[i] for i in range(count)])
+        if relays:
+            pl.semaphore_wait(relay, len(relays))
+        for j in column:
+            send(1, got_column, j, column_at(j, 0))
+            if j:
+                send(1, got_column, j - 1, column_at(j, 1))
+
     row8 = row_of((8, LANES))
-    for copy in curve_copies:
-        copy.wait_recv()
+
+    @pl.when(jnp.logical_not(last))
+    def _():
+        for copy in to_before:
+            copy.wait_recv()
+
+    @pl.when(jnp.logical_not(first))
+    def _():
+        for copy in to_after:
+            copy.wait_recv()
+
     for z in range(DEPTH):
         fourth, sides = [], []
         for f in range(7):
@@ -224,9 +277,11 @@
             ext[6, 2 + z, i * 8 : i * 8 + 8] = 0.5 * group[6]
 
     plane_copies = [
-        halo(3, ext.at[:, pl.ds(4, 2)], low_planes, near_at(1)),
-        halo(4, ext.at[:, pl.ds(2, 2)], high_planes, near_at(n_near - 1)),
+        halo(3, ext.at[:, pl.ds(4, 2)], low_planes, (curve, lax.rem(near + 1, n_near))),
+        halo(4, ext.at[:, pl.ds(2, 2)], high_planes, (curve, lax.rem(near + n_near - 1, n_near))),
     ]
+    for copy in plane_copies:
+        copy.start()
 
     def fill_derived(z):
         for i, value in enumerate(derive([ext[f, z] for f in range(5)])):
@@ -240,10 +295,6 @@
             rate_out[f, z - 1] = value
 
     lax.fori_loop(2, 6, lambda z, c: (fill_derived(z), c)[1], 0)
-
-    best = gathered(y_copies, got_y, best)
-    sent[2] = best
-    z_copies = exchange(2, got_z, z_at, n_z, z_send, z_recv)
 
     lax.fori_loop(3, 5, lambda z, c: (fill_rate(z), c)[1], 0)
 
@@ -261,11 +312,30 @@
         for z in range(6):
             u_out[f, z] = ext[f, z + 1]
     flag_out[0:1] = flag_sent[...]
-    flag_out[1:2] = flag_got[...]
-
-    top_out[...] = gathered(z_copies, got_z, best)
-    for copy in near_copies + curve_copies + y_copies + z_copies:
-        copy.wait_send()
+    flag_out[1:2] = jnp.where(last, 0.0, flag_got[...])
+
+    @pl.when(jnp.logical_not(first))
+    def _():
+        for copy in to_before:
+            copy.wait_send()
+
+    @pl.when(jnp.logical_not(last))
+    def _():
+        for copy in to_after:
+            copy.wait_send()
+
+    @pl.when(core == 0)
+    def _():
+        wait_rows(stage_send.at[0], got_plane, n_plane)
+        wait_rows(stage_recv.at[1], got_column, n_z)
+        top_out[...] = largest([got_column[i] for i in range(n_z)])
+
+    @pl.when(core == 1)
+    def _():
+        wait_rows(stage_send.at[0], got_plane, n_plane - 1)
+        wait_rows(stage_recv.at[1], got_column, n_z - 1)
+        top_out[...] = largest([sent[1]] + [got_column[i] for i in range(n_z - 1)])
+        wait_rows(stage_send.at[1], got_plane, 2 * n_z - 1)
 
 
 def finish_kernel(n_curve, u_ref, rate_ref, top_ref, flag_ref, out_ref, half, der):
@@ -340,18 +410,18 @@
             pltpu.VMEM((6, 8, ROWS, LANES), F32),
             pltpu.VMEM((7, 2, ROWS, LANES), F32),
             pltpu.VMEM((7, 2, ROWS, LANES), F32),
-            pltpu.VMEM((3, 1, LANES), F32),
-            pltpu.VMEM((n_near - 1, 1, LANES), F32),
-            pltpu.VMEM((n_y - 1, 1, LANES), F32),
-            pltpu.VMEM((n_z - 1, 1, LANES), F32),
+            pltpu.VMEM((2, 1, LANES), F32),
+            pltpu.VMEM((max(n_near * n_y - 1, 2 * n_z - 1), 1, LANES), F32),
+            pltpu.VMEM((n_z, 1, LANES), F32),
             pltpu.VMEM((1, LANES), F32),
             pltpu.VMEM((1, LANES), F32),
             pltpu.SMEM((BOXES,), jnp.int32),
             dma((3,)),
-            dma((n_near - 1,)), dma((n_near - 1,)),
-            dma((n_y - 1,)), dma((n_y - 1,)),
-            dma((n_z - 1,)), dma((n_z - 1,)),
-            dma((5,)), dma((5,)),
+            dma((2,)),
+            dma((2,)),
+            dma((5,)),
+            dma((5,)),
+            pltpu.SemaphoreType.REGULAR,
         ],
         compiler_params=pltpu.CompilerParams(collective_id=0, has_side_effects=True),
         name="exchange",

time: 36.4 us -> 33.1 us (0.909)
  Pallas kernels: 36.2 us -> 32.9 us
    pallas_call x1, Pallas kernels: 33 us -> 29.7 us  [local(): pl.pallas_call(functools.partial(exchange_kernel, n_curve, n_near), out_s...]
where the time goes in v2:
time: 33.1 us; the launch traced here: 32.9 us
  Pallas kernels  32.9 us (99%)
    pallas_call x1, Pallas kernels, local(): pl.pallas_call(functools.partial(exchange_kernel, n_curve, n_near), out_s...  29.7 us
    pallas_call x1, Pallas kernels, local(): pl.pallas_call(functools.partial(finish_kernel, n_curve), out_shape=jax.S...  3.2 us

profile of v2, /device:TPU:1, one launch (start us, length us, event | category | flops | bytes accessed | tf_op | source)
XLA Modules:
  0.0 32.9 jit_solution(6125751179057277658)
XLA Ops:
  0.0 29.7 %exchange.1 = (f32[7,6,40,128]{3,2,1,0:T(8,128)S(1)}, f32[6,6,40,128]{3,2,1,0:T(8,128)S(1)}, f32[1,128]{1,0:T(1,128)S(1)}, f32[2,128]{1,0:T(2,128)S(1)}) custom-call(f32[6,96,128]{2,1,0:T(8,128)} %bitcast.15, f32[96,128]{1,0:T(8,128)} %bitcast.16, s32[3]{0:T(128)} %owner_hbm.1), custom_call_target="tpu_custom_call" | custom-call | tf_op jit(solution)/shard_map/exchange/pallas_call | solution.py:395
  29.7 3.2 %finish.1 = f32[6,128,128]{2,1,0:T(8,128)} custom-call(f32[7,6,40,128]{3,2,1,0:T(8,128)S(1)} %get-tuple-element.9.u_ref, f32[6,6,40,128]{3,2,1,0:T(8,128)S(1)} %get-tuple-element.10.rate_ref, f32[1,128]{1,0:T(1,128)S(1)} %get-tuple-element.11.top_ref, f32[2,128]{1,0:T(2,128)S(1)} %get-tuple-element.12.flag_ref), custom_call_target="tpu_custom_call" | custom-call | tf_op jit(solution)/shard_map/finish/pallas_call | solution.py:429

commit v3 on v2

--- a/solution.py
+++ b/solution.py
@@ -16,6 +16,7 @@
 NEXT = 40
 PREV = 8
 Y_CHIPS = 8
+VMEM_LIMIT = 48 << 20
 RELAY = 3
 MESH = pl.DeviceIdType.MESH
 F32 = jnp.float32
@@ -102,7 +103,7 @@
 def exchange_kernel(
     n_curve, n_near,
     prim_hbm, cond_hbm, owner_hbm,
-    u_out, rate_out, top_out, flag_out,
+    u_out, rate_out, u_side, rate_side, top_out, flag_out,
     raw, from_next, from_prev, ext, der, low_planes, high_planes,
     sent, got_plane, got_column, flag_sent, flag_got, owner,
     load_sem, stage_send, stage_recv, halo_send, halo_recv, relay,
@@ -290,9 +291,22 @@
     def cell(z):
         return [ext[f, z] for f in range(6)], [der[i, z] for i in range(6)], ext[6, z]
 
+    row = row_of((ROWS, LANES))
+    left_edge = jnp.logical_and(first, row == ROWS - 1)
+    right_edge = jnp.logical_and(last, row == OWN)
+
     def fill_rate(z):
         for f, value in enumerate(plane_rate(cell, z)):
-            rate_out[f, z - 1] = value
+            left = pltpu.roll(jnp.broadcast_to(value[0:1], value.shape), LANES - BW, 1)
+            right = pltpu.roll(jnp.broadcast_to(value[OWN - 1 : OWN], value.shape), BW, 1)
+            rate_out[f, z - 1] = jnp.where(right_edge, right, jnp.where(left_edge, left, value))
+
+    def fill_sides(z):
+        lane = lane_of((ROWS, LANES))
+        for f in range(7):
+            for ref, of in ((u_side, ext[f, z + 2]),) + (((rate_side, rate_out[f, z + 1]),) if f < 6 else ()):
+                ref[0, f, z] = upper_x(of, lane)
+                ref[1, f, z] = upper_y(of, lane % BW)
 
     lax.fori_loop(2, 6, lambda z, c: (fill_derived(z), c)[1], 0)
 
@@ -308,6 +322,7 @@
         fill_derived(z)
     lax.fori_loop(0, 2, lambda i, c: (fill_rate(1 + 4 * i), c)[1], 0)
     lax.fori_loop(0, 2, lambda i, c: (fill_rate(2 + 4 * i), c)[1], 0)
+    lax.fori_loop(0, DEPTH, lambda z, c: (fill_sides(z), c)[1], 0)
     for f in range(7):
         for z in range(6):
             u_out[f, z] = ext[f, z + 1]
@@ -338,47 +353,117 @@
         wait_rows(stage_send.at[1], got_plane, 2 * n_z - 1)
 
 
-def finish_kernel(n_curve, u_ref, rate_ref, top_ref, flag_ref, out_ref, half, der):
-    curve = lax.axis_index("curve")
-    first, last = curve == 0, curve == n_curve - 1
+def beside_y(v, by):
+    lane = lane_of(v.shape)
+    wanted = lane - lane % BW + (lane + by) % BW
+    return jnp.take_along_axis(v, wanted, axis=1, mode="promise_in_bounds")
+
+
+def with_pressure(u, w, c, k):
+    temp = c * c
+    return u, w, c, k, temp, u[0] * (temp * (0.5 / 0.35))
+
+
+def second_face(lo, hi, k):
+    (lu, lw, lc, lk, lt, lp), (hu, hw, hc, hk, ht, hp) = lo, hi
+    top = jnp.maximum(jnp.abs(lw) + lc, jnp.abs(hw) + hc)
+    lf, hf = lw + top, hw - top
+    flux = [a * lf + b * hf for a, b in zip(lu, hu)]
+    flux[1 + k] = flux[1 + k] + (lp + hp)
+    work = lp * lw + hp * hw
+    flux[4] = flux[4] + (work + work) - ((lk + hk) * (1.0 / 0.35)) * (ht - lt)
+    return flux
+
+
+def finish_kernel(u_ref, rate_ref, u_side, rate_side, top_ref, flag_ref, out_ref, half, der, low_faces):
     top = top_ref[...]
     lane = lane_of(top.shape)
     speed = jnp.max(jnp.where(lane < LANES // 2, top, 0.0), axis=1, keepdims=True)
     cond = jnp.max(jnp.where(lane < LANES // 2, 0.0, top), axis=1, keepdims=True)
-    step = 0.8 / (speed + 6.0 * cond)
-    row = row_of((ROWS, LANES))
+    step = jnp.broadcast_to(0.8 / (speed + 6.0 * cond), (8, LANES))
+    chunks = ROWS // 8
+    lane, row = lane_of((8, LANES)), row_of((8, LANES))
 
     def fill_half(z, carry):
-        values = []
-        for f in range(6):
-            v = u_ref[f, z] + step * rate_ref[f, z]
-            left = pltpu.roll(jnp.broadcast_to(v[0:1], v.shape), LANES - BW, 1)
-            right = pltpu.roll(jnp.broadcast_to(v[OWN - 1 : OWN], v.shape), BW, 1)
-            v = jnp.where(jnp.logical_and(first, row == ROWS - 1), left, v)
-            v = jnp.where(jnp.logical_and(last, row == OWN), right, v)
-            half[f, z] = v
-            values.append(v)
-        for i, value in enumerate(derive(values[:5])):
-            der[i, z] = value
+        for i in range(chunks):
+            rows = pl.ds(8 * i, 8)
+            values = [u_ref[f, z, rows] + step * rate_ref[f, z, rows] for f in range(6)]
+            for f in range(6):
+                half[f, z, rows] = values[f]
+            for k, value in enumerate(derive(values[:5])[:4]):
+                der[k, z, rows] = value
         return carry
 
     lax.fori_loop(0, 6, fill_half, 0)
     leaving = flag_ref[0:1] > 0.5
     arriving = flag_ref[1:2] > 0.5
-
-    def cell(z):
-        return [half[f, z] for f in range(6)], [der[i, z] for i in range(6)], u_ref[6, z]
+    emptied = jnp.logical_and(leaving, jnp.logical_not(arriving))
+    filled = jnp.logical_and(arriving, jnp.logical_not(leaving))
+    half_step = 0.5 * step
+
+    def fields(z, i):
+        return [half[f, z, pl.ds(8 * i, 8)] for f in range(6)]
+
+    def chunk(z, i, k, u):
+        rows = pl.ds(8 * i, 8)
+        return with_pressure(u, der[k, z, rows], der[3, z, rows], u_ref[6, z, rows])
+
+    def side(k, z, i, w, c):
+        rows = pl.ds(8 * i, 8)
+        u = [u_side[k, f, z - 1, rows] + step * rate_side[k, f, z - 1, rows] for f in range(6)]
+        return with_pressure(u, w, c, u_side[k, 6, z - 1, rows])
+
+    def x_faces(z, i, u):
+        def beside(k):
+            if i == chunks - 1:
+                above = jnp.broadcast_to(der[k, z, 0:1], (8, LANES))
+            else:
+                above = der[k, z, pl.ds(8 * i + 1, 8)]
+            return pltpu.roll(jnp.where(lane < BW, above, der[k, z, pl.ds(8 * i, 8)]), LANES - BW, 1)
+
+        return second_face(chunk(z, i, 0, u), side(0, z, i, beside(0), beside(3)), 0)
+
+    def y_faces(z, i, u):
+        rows = pl.ds(8 * i, 8)
+        w, c = beside_y(der[1, z, rows], 1), beside_y(der[3, z, rows], 1)
+        return second_face(chunk(z, i, 1, u), side(1, z, i, w, c), 1)
+
+    def z_faces(z, i, u):
+        return second_face(chunk(z, i, 2, u), chunk(z + 1, i, 2, fields(z + 1, i)), 2)
+
+    for i in range(BOXES + 1):
+        for f, value in enumerate(z_faces(0, i, fields(0, i))):
+            low_faces[f, i] = value
 
     def fill_out(z, carry):
-        rates = plane_rate(cell, z)
-        for f in range(6):
-            final = 0.5 * u_ref[f, z] + 0.5 * (half[f, z] + step * rates[f])
-            box = [final[8 * j : 8 * j + 8] for j in range(BOXES + 1)]
-            slot = [jnp.where(leaving, box[j + 1], box[j]) for j in range(BOXES)]
-            slot[2] = jnp.where(jnp.logical_and(leaving, jnp.logical_not(arriving)), 0.0, slot[2])
-            slot.append(jnp.where(jnp.logical_and(arriving, jnp.logical_not(leaving)), box[3], 0.0))
-            for j, value in enumerate(slot):
-                out_ref[f, pl.ds(j * 8 * DEPTH + z - 1, 8, stride=DEPTH)] = value
+        below = [pltpu.roll(f, 1, 0) for f in x_faces(z, chunks - 1, fields(z, chunks - 1))]
+        uppers, finals = [], []
+        for i in range(BOXES + 1):
+            u = fields(z, i)
+            flux = x_faces(z, i, u)
+            turned = [pltpu.roll(f, 1, 0) for f in flux]
+            total = []
+            for f in range(6):
+                lower = jnp.where(row == 0, below[f], turned[f])
+                total.append(pltpu.roll(jnp.where(lane >= LANES - BW, lower, flux[f]), BW, 1) - flux[f])
+            below = turned
+            flux = y_faces(z, i, u)
+            total = [t + (beside_y(f, BW - 1) - f) for t, f in zip(total, flux)]
+            flux = z_faces(z, i, u)
+            uppers.append(flux)
+            finals.append([
+                0.5 * (u_ref[f, z, pl.ds(8 * i, 8)] + u[f]) + half_step * (total[f] + (low_faces[f, i] - flux[f]))
+                for f in range(6)
+            ])
+        for i in range(BOXES + 1):
+            for f in range(6):
+                low_faces[f, i] = uppers[i][f]
+                if i < BOXES:
+                    value = jnp.where(leaving, finals[i + 1][f], finals[i][f])
+                    value = jnp.where(emptied, 0.0, value) if i == BOXES - 1 else value
+                else:
+                    value = jnp.where(filled, finals[i][f], 0.0)
+                out_ref[f, pl.ds(i * 8 * DEPTH + z - 1, 8, stride=DEPTH)] = value
         return carry
 
     lax.fori_loop(1, 5, fill_out, 0)
@@ -389,7 +474,7 @@
     prim = primitive.reshape(6, DEPTH, OWN, LANES).transpose(0, 2, 1, 3).reshape(6, rows, LANES)
     cond = conductivity.reshape(DEPTH, OWN, LANES).transpose(1, 0, 2).reshape(rows, LANES)
     n_y, n_z = Y_CHIPS, n_curve // Y_CHIPS
-    anywhere = pl.BlockSpec(memory_space=pl.ANY)
+    hbm = pl.BlockSpec(memory_space=pltpu.HBM)
     vmem = pl.BlockSpec(memory_space=pltpu.VMEM)
     dma = pltpu.SemaphoreType.DMA
     state = pl.pallas_call(
@@ -397,11 +482,13 @@
         out_shape=(
             pltpu.VMEM((7, 6, ROWS, LANES), F32),
             pltpu.VMEM((6, 6, ROWS, LANES), F32),
+            pltpu.VMEM((2, 7, DEPTH, ROWS, LANES), F32),
+            pltpu.VMEM((2, 6, DEPTH, ROWS, LANES), F32),
             pltpu.VMEM((1, LANES), F32),
             pltpu.VMEM((2, LANES), F32),
         ),
-        in_specs=[anywhere] * 3,
-        out_specs=(vmem,) * 4,
+        in_specs=[hbm] * 3,
+        out_specs=(vmem,) * 6,
         scratch_shapes=[
             pltpu.VMEM((7, rows, LANES), F32),
             pltpu.VMEM((7, NEXT, LANES), F32),
@@ -423,15 +510,20 @@
             dma((5,)),
             pltpu.SemaphoreType.REGULAR,
         ],
-        compiler_params=pltpu.CompilerParams(collective_id=0, has_side_effects=True),
+        compiler_params=pltpu.CompilerParams(collective_id=0, has_side_effects=True, vmem_limit_bytes=VMEM_LIMIT),
         name="exchange",
-    )(prim, cond, new_owner)
+    )(*(pltpu.with_memory_space_constraint(v, pltpu.HBM) for v in (prim, cond, new_owner)))
     out = pl.pallas_call(
-        functools.partial(finish_kernel, n_curve),
+        finish_kernel,
         out_shape=jax.ShapeDtypeStruct((6, 32 * DEPTH, LANES), F32),
-        in_specs=[vmem] * 4,
+        in_specs=[vmem] * 6,
         out_specs=vmem,
-        scratch_shapes=[pltpu.VMEM((6, 6, ROWS, LANES), F32)] * 2,
+        scratch_shapes=[
+            pltpu.VMEM((6, 6, ROWS, LANES), F32),
+            pltpu.VMEM((4, 6, ROWS, LANES), F32),
+            pltpu.VMEM((6, BOXES + 1, 8, LANES), F32),
+        ],
+        compiler_params=pltpu.CompilerParams(vmem_limit_bytes=VMEM_LIMIT),
         name="finish",
     )(*(pltpu.with_memory_space_constraint(v, pltpu.VMEM) for v in state))
     out = out.reshape(6, 32, DEPTH, LANES).transpose(0, 2, 1, 3).reshape(6, DEPTH, 32 * LANES)

time: 33.1 us -> 33.1 us (level)
    pallas_call x1, Pallas kernels: 3.2 us -> 2.07 us  [local(): pl.pallas_call(finish_kernel, out_shape=jax.ShapeDtypeStruct((6, 32 * DEP...]
    pallas_call x1, Pallas kernels: 29.7 us -> 30.8 us  [local(): pl.pallas_call(functools.partial(exchange_kernel, n_curve, n_near), out_s...]
where the time goes in v3:
time: 33.1 us; the launch traced here: 32.9 us
  Pallas kernels  32.9 us (99%)
    pallas_call x1, Pallas kernels, local(): pl.pallas_call(functools.partial(exchange_kernel, n_curve, n_near), out_s...  30.8 us
    pallas_call x1, Pallas kernels, local(): pl.pallas_call(finish_kernel, out_shape=jax.ShapeDtypeStruct((6, 32 * DEP...  2.07 us

profile of v3, /device:TPU:1, one launch (start us, length us, event | category | flops | bytes accessed | tf_op | source)
XLA Modules:
  0.0 32.9 jit_solution(133609504553187519)
XLA Ops:
  0.0 30.8 %exchange.1 = (f32[7,6,40,128]{3,2,1,0:T(8,128)S(1)}, f32[6,6,40,128]{3,2,1,0:T(8,128)S(1)}, f32[2,7,4,40,128]{4,3,2,1,0:T(8,128)S(1)}, f32[2,6,4,40,128]{4,3,2,...) custom-call(f32[6,96,128]{2,1,0:T(8,128)} %bitcast.15, f32[96,128]{1,0:T(8,128)} %bitcast.16, s32[3]{0:T(128)} %owner_hbm.1), custom_call_target="tpu_custom_call" | custom-call | tf_op jit(solution)/shard_map/exchange/pallas_call | solution.py:480
  30.9 2.1 %finish.1 = f32[6,128,128]{2,1,0:T(8,128)} custom-call(f32[7,6,40,128]{3,2,1,0:T(8,128)S(1)} %get-tuple-element.11.u_ref, f32[6,6,40,128]{3,2,1,0:T(8,128)S(1)} %get-tuple-element.12.rate_ref, f32[2,7,4,40,128]{4,3,2,1,0:T(8,128)S(1)} %get-tuple-element.13.u_side, f32[2,6,4,40,128]{4,3,2,1,0:T(8,128)S(1)} %get-tuple-element.14.rate_side, ...), custom_call_target="tpu_custom_call" | custom-call | tf_op jit(solution)/shard_map/finish/pallas_call | solution.py:516

commit v4 on v3

--- a/solution.py
+++ b/solution.py
@@ -126,13 +126,17 @@
 
     ys = [lax.rem(y + j, n_y) for j in range(n_y)]
     xs = [2 * lax.rem(x + j, n_x) for j in range(n_x)]
-    zs = [n_y * lax.rem(z_chip + j, n_z) for j in range(n_z)]
 
     def plane_at(offset, side):
-        return (zs[0] + ys[offset[1]], xs[offset[0]] + side)
-
-    def column_at(j, side):
-        return (zs[j] + ys[0], xs[0] + side)
+        return (n_y * z_chip + ys[offset[1]], xs[offset[0]] + side)
+
+    def column_at(to, side):
+        return (n_y * to + y, 2 * x + side)
+
+    def for_close(act):
+        for d in range(1, min(RELAY, n_z - 1) + 1):
+            pl.when(z_chip >= d)(functools.partial(act, z_chip - d))
+            pl.when(z_chip + d < n_z)(functools.partial(act, z_chip + d))
 
     plane = sorted(
         ((i, j) for i in range(n_x) for j in range(n_y)),
@@ -141,9 +145,6 @@
     slot_of = {o: o[0] * n_y + o[1] for o in plane}
     others = [o for o in plane if slot_of[o] > 0]
     n_plane = len(plane)
-    column = sorted(range(n_z), key=lambda j: -ring(j, n_z))
-    close = [j for j in column if 0 < ring(j, n_z) <= RELAY]
-    relays = [RELAY, n_z - RELAY] if n_z // 2 > RELAY else []
     before, after = (lax.rem(curve + n_curve - 1, n_curve), near), (lax.rem(curve + 1, n_curve), near)
     barrier = pltpu.get_barrier_semaphore()
 
@@ -153,14 +154,15 @@
 
     @pl.when(core == 0)
     def _():
-        greet([plane_at(o, 1) for o in plane] + [column_at(j, 1) for j in close])
+        greet([plane_at(o, 1) for o in plane])
 
     @pl.when(core == 1)
     def _():
         greet([plane_at(o, 1) for o in others] + [plane_at(o, 0) for o in plane])
-        greet([column_at(j, 1) for j in close])
-
-    greet([before, after])
+
+    pl.when(jnp.logical_not(first))(lambda: greet([before]))
+    pl.when(jnp.logical_not(last))(lambda: greet([after]))
+    for_close(lambda to: greet([column_at(to, 1)]))
 
     for copy in loads:
         copy.wait()
@@ -203,20 +205,46 @@
             device_id=device, device_id_type=MESH,
         )
 
+    sides = lax.div(curve + n_curve - 1, n_curve) + 1 - lax.div(curve + 1, n_curve)
+    contacts = 0
+    for d in range(1, min(RELAY, n_z - 1) + 1):
+        contacts = contacts + lax.div(z_chip - d + n_z, n_z) + 1 - lax.div(z_chip + d, n_z)
+
     @pl.when(core == 0)
     def _():
-        pl.semaphore_wait(barrier, n_plane + 2)
+        pl.semaphore_wait(barrier, n_plane + sides)
         for o in plane:
             send(0, got_plane, n_plane - 1 + slot_of[o], plane_at(o, 1))
 
     @pl.when(core == 1)
     def _():
-        pl.semaphore_wait(barrier, 2 * n_plane - 1 + 2 * len(close) + 2)
-        for j in relays:
-            pl.semaphore_signal(relay, inc=1, device_id=column_at(j, 1), device_id_type=MESH)
+        pl.semaphore_wait(barrier, 2 * n_plane - 1 + 2 * contacts + sides)
         for o in others:
             send(0, got_plane, slot_of[o] - 1, plane_at(o, 1))
 
+    def pass_on(sem, source, target):
+        inside = (source >= 0, source < n_z), (target >= 0, target < n_z)
+        pl.when(jnp.logical_and(*inside[0]))(lambda: pl.semaphore_wait(sem, 1))
+        pl.when(jnp.logical_and(*inside[1]))(
+            lambda: pl.semaphore_signal(sem, inc=1, device_id=column_at(target, 1), device_id_type=MESH)
+        )
+
+    def send_column(to):
+        slot = lax.rem(to - z_chip + n_z, n_z)
+        send(1, got_column, slot, column_at(to, 0))
+        send(1, got_column, slot - 1, column_at(to, 1))
+
+    def finish_column():
+        pass_on(relay.at[1], z_chip + RELAY, z_chip - RELAY)
+
+    def send_above():
+        lax.fori_loop(z_chip + RELAY + 1, n_z, lambda to, c: (send_column(to), c)[1], 0)
+
+    on_core = core == 1
+    at_once = jnp.logical_and(on_core, z_chip + 2 * RELAY >= n_z)
+    soon = jnp.logical_and(on_core, jnp.logical_and(z_chip >= RELAY, z_chip + 2 * RELAY < n_z))
+    at_last = jnp.logical_and(on_core, jnp.logical_and(z_chip < RELAY, z_chip + 2 * RELAY < n_z))
+
     to_before = [halo(0, raw.at[:, pl.ds(0, NEXT)], from_next, before), halo(2, flag_sent, flag_got, before)]
     to_after = [halo(1, raw.at[:, pl.ds(raw.shape[1] - PREV, PREV)], from_prev, after)]
 
@@ -229,6 +257,9 @@
     def _():
         for copy in to_after:
             copy.start()
+
+    pl.when(on_core)(lambda: pass_on(relay.at[0], z_chip - RELAY, z_chip + RELAY))
+    pl.when(at_once)(finish_column)
 
     for z in range(DEPTH):
         for i in range(OWN // 8):
@@ -242,12 +273,17 @@
         count = 2 * n_plane - 1
         wait_rows(stage_recv.at[0], got_plane, count)
         sent[1] = largest([sent[0]] + [got_plane[i] for i in range(count)])
-        if relays:
-            pl.semaphore_wait(relay, len(relays))
-        for j in column:
-            send(1, got_column, j, column_at(j, 0))
-            if j:
-                send(1, got_column, j - 1, column_at(j, 1))
+        lax.fori_loop(0, z_chip, lambda to, c: (send_column(to), c)[1], 0)
+        send(1, got_column, 0, column_at(z_chip, 0))
+        for d in range(1, min(RELAY, n_z - 1) + 1):
+            pl.when(z_chip + d < n_z)(functools.partial(send_column, z_chip + d))
+
+    pl.when(at_once)(send_above)
+
+    @pl.when(soon)
+    def _():
+        finish_column()
+        send_above()
 
     row8 = row_of((8, LANES))
 
@@ -326,6 +362,12 @@
     for f in range(7):
         for z in range(6):
             u_out[f, z] = ext[f, z + 1]
+
+    @pl.when(at_last)
+    def _():
+        finish_column()
+        send_above()
+
     flag_out[0:1] = flag_sent[...]
     flag_out[1:2] = jnp.where(last, 0.0, flag_got[...])
 
@@ -508,7 +550,7 @@
             dma((2,)),
             dma((5,)),
             dma((5,)),
-            pltpu.SemaphoreType.REGULAR,
+            pltpu.SemaphoreType.REGULAR((2,)),
         ],
         compiler_params=pltpu.CompilerParams(collective_id=0, has_side_effects=True, vmem_limit_bytes=VMEM_LIMIT),
         name="exchange",

time: 33.1 us -> 31.7 us (0.958)
  Pallas kernels: 32.9 us -> 31.5 us
    pallas_call x1, Pallas kernels: 30.8 us -> 29.5 us  [local(): pl.pallas_call(functools.partial(exchange_kernel, n_curve, n_near), out_s...]
where the time goes in v4:
time: 31.7 us; the launch traced here: 31.6 us
  Pallas kernels  31.5 us (99%)
    pallas_call x1, Pallas kernels, local(): pl.pallas_call(functools.partial(exchange_kernel, n_curve, n_near), out_s...  29.5 us
    pallas_call x1, Pallas kernels, local(): pl.pallas_call(finish_kernel, out_shape=jax.ShapeDtypeStruct((6, 32 * DEP...  2.07 us

profile of v4, /device:TPU:1, one launch (start us, length us, event | category | flops | bytes accessed | tf_op | source)
XLA Modules:
  0.0 31.6 jit_solution(14306888246794234844)
XLA Ops:
  0.0 29.5 %exchange.1 = (f32[7,6,40,128]{3,2,1,0:T(8,128)S(1)}, f32[6,6,40,128]{3,2,1,0:T(8,128)S(1)}, f32[2,7,4,40,128]{4,3,2,1,0:T(8,128)S(1)}, f32[2,6,4,40,128]{4,3,2,...) custom-call(f32[6,96,128]{2,1,0:T(8,128)} %bitcast.15, f32[96,128]{1,0:T(8,128)} %bitcast.16, s32[3]{0:T(128)} %owner_hbm.1), custom_call_target="tpu_custom_call" | custom-call | tf_op jit(solution)/shard_map/exchange/pallas_call | solution.py:522
  29.5 2.1 %finish.1 = f32[6,128,128]{2,1,0:T(8,128)} custom-call(f32[7,6,40,128]{3,2,1,0:T(8,128)S(1)} %get-tuple-element.11.u_ref, f32[6,6,40,128]{3,2,1,0:T(8,128)S(1)} %get-tuple-element.12.rate_ref, f32[2,7,4,40,128]{4,3,2,1,0:T(8,128)S(1)} %get-tuple-element.13.u_side, f32[2,6,4,40,128]{4,3,2,1,0:T(8,128)S(1)} %get-tuple-element.14.rate_side, ...), custom_call_target="tpu_custom_call" | custom-call | tf_op jit(solution)/shard_map/finish/pallas_call | solution.py:558

commit v5 on v4

--- a/solution.py
+++ b/solution.py
@@ -158,7 +158,7 @@
 
     @pl.when(core == 1)
     def _():
-        greet([plane_at(o, 1) for o in others] + [plane_at(o, 0) for o in plane])
+        greet([plane_at(o, side) for o in plane for side in (0, 1) if side == 0 or slot_of[o]])
 
     pl.when(jnp.logical_not(first))(lambda: greet([before]))
     pl.when(jnp.logical_not(last))(lambda: greet([after]))
@@ -426,17 +426,17 @@
     chunks = ROWS // 8
     lane, row = lane_of((8, LANES)), row_of((8, LANES))
 
-    def fill_half(z, carry):
-        for i in range(chunks):
+    def fill_half(z, count):
+        for i in range(count):
             rows = pl.ds(8 * i, 8)
             values = [u_ref[f, z, rows] + step * rate_ref[f, z, rows] for f in range(6)]
             for f in range(6):
                 half[f, z, rows] = values[f]
             for k, value in enumerate(derive(values[:5])[:4]):
                 der[k, z, rows] = value
-        return carry
-
-    lax.fori_loop(0, 6, fill_half, 0)
+
+    lax.fori_loop(0, 2, lambda j, c: (fill_half(5 * j, BOXES + 1), c)[1], 0)
+    lax.fori_loop(1, 5, lambda z, c: (fill_half(z, chunks), c)[1], 0)
     leaving = flag_ref[0:1] > 0.5
     arriving = flag_ref[1:2] > 0.5
     emptied = jnp.logical_and(leaving, jnp.logical_not(arriving))

time: 31.7 us -> 31.7 us (level)
  no operation moved by 1% of the time
where the time goes in v5:
time: 31.7 us; the launch traced here: 31.5 us
  Pallas kernels  31.5 us (99%)
    pallas_call x1, Pallas kernels, local(): pl.pallas_call(functools.partial(exchange_kernel, n_curve, n_near), out_s...  29.5 us
    pallas_call x1, Pallas kernels, local(): pl.pallas_call(finish_kernel, out_shape=jax.ShapeDtypeStruct((6, 32 * DEP...  2.06 us

profile of v5, /device:TPU:1, one launch (start us, length us, event | category | flops | bytes accessed | tf_op | source)
XLA Modules:
  0.0 31.5 jit_solution(2575283240962919375)
XLA Ops:
  0.0 29.5 %exchange.1 = (f32[7,6,40,128]{3,2,1,0:T(8,128)S(1)}, f32[6,6,40,128]{3,2,1,0:T(8,128)S(1)}, f32[2,7,4,40,128]{4,3,2,1,0:T(8,128)S(1)}, f32[2,6,4,40,128]{4,3,2,...) custom-call(f32[6,96,128]{2,1,0:T(8,128)} %bitcast.15, f32[96,128]{1,0:T(8,128)} %bitcast.16, s32[3]{0:T(128)} %owner_hbm.1), custom_call_target="tpu_custom_call" | custom-call | tf_op jit(solution)/shard_map/exchange/pallas_call | solution.py:522
  29.5 2.1 %finish.1 = f32[6,128,128]{2,1,0:T(8,128)} custom-call(f32[7,6,40,128]{3,2,1,0:T(8,128)S(1)} %get-tuple-element.11.u_ref, f32[6,6,40,128]{3,2,1,0:T(8,128)S(1)} %get-tuple-element.12.rate_ref, f32[2,7,4,40,128]{4,3,2,1,0:T(8,128)S(1)} %get-tuple-element.13.u_side, f32[2,6,4,40,128]{4,3,2,1,0:T(8,128)S(1)} %get-tuple-element.14.rate_side, ...), custom_call_target="tpu_custom_call" | custom-call | tf_op jit(solution)/shard_map/finish/pallas_call | solution.py:558

commit v6 on v4

--- a/solution.py
+++ b/solution.py
@@ -164,7 +164,7 @@
     pl.when(jnp.logical_not(last))(lambda: greet([after]))
     for_close(lambda to: greet([column_at(to, 1)]))
 
-    for copy in loads:
+    for copy in loads[:2]:
         copy.wait()
     speed, cond = None, None
     for i in range(0, raw.shape[1], 8):
@@ -181,8 +181,6 @@
     )
     best = jnp.max(both, axis=0, keepdims=True)
     sent[0] = best
-    leaving = jnp.where(owner[0] != curve, 1.0, 0.0).astype(F32)
-    flag_sent[...] = jnp.full(flag_sent.shape, leaving, F32)
 
     def send(stage, got, slot, device):
         pltpu.make_async_remote_copy(
@@ -245,6 +243,9 @@
     soon = jnp.logical_and(on_core, jnp.logical_and(z_chip >= RELAY, z_chip + 2 * RELAY < n_z))
     at_last = jnp.logical_and(on_core, jnp.logical_and(z_chip < RELAY, z_chip + 2 * RELAY < n_z))
 
+    loads[2].wait()
+    leaving = jnp.where(owner[0] != curve, 1.0, 0.0).astype(F32)
+    flag_sent[...] = jnp.full(flag_sent.shape, leaving, F32)
     to_before = [halo(0, raw.at[:, pl.ds(0, NEXT)], from_next, before), halo(2, flag_sent, flag_got, before)]
     to_after = [halo(1, raw.at[:, pl.ds(raw.shape[1] - PREV, PREV)], from_prev, after)]
 

time: 31.7 us -> 31.7 us (level)
  no operation moved by 1% of the time
where the time goes in v6:
time: 31.7 us; the launch traced here: 31.6 us
  Pallas kernels  31.6 us (100%)
    pallas_call x1, Pallas kernels, local(): pl.pallas_call(functools.partial(exchange_kernel, n_curve, n_near), out_s...  29.5 us
    pallas_call x1, Pallas kernels, local(): pl.pallas_call(finish_kernel, out_shape=jax.ShapeDtypeStruct((6, 32 * DEP...  2.07 us

profile of v6, /device:TPU:1, one launch (start us, length us, event | category | flops | bytes accessed | tf_op | source)
XLA Modules:
  0.0 31.6 jit_solution(9478088525409321655)
XLA Ops:
  0.0 29.5 %exchange.1 = (f32[7,6,40,128]{3,2,1,0:T(8,128)S(1)}, f32[6,6,40,128]{3,2,1,0:T(8,128)S(1)}, f32[2,7,4,40,128]{4,3,2,1,0:T(8,128)S(1)}, f32[2,6,4,40,128]{4,3,2,...) custom-call(f32[6,96,128]{2,1,0:T(8,128)} %bitcast.15, f32[96,128]{1,0:T(8,128)} %bitcast.16, s32[3]{0:T(128)} %owner_hbm.1), custom_call_target="tpu_custom_call" | custom-call | tf_op jit(solution)/shard_map/exchange/pallas_call | solution.py:523
  29.5 2.1 %finish.1 = f32[6,128,128]{2,1,0:T(8,128)} custom-call(f32[7,6,40,128]{3,2,1,0:T(8,128)S(1)} %get-tuple-element.11.u_ref, f32[6,6,40,128]{3,2,1,0:T(8,128)S(1)} %get-tuple-element.12.rate_ref, f32[2,7,4,40,128]{4,3,2,1,0:T(8,128)S(1)} %get-tuple-element.13.u_side, f32[2,6,4,40,128]{4,3,2,1,0:T(8,128)S(1)} %get-tuple-element.14.rate_side, ...), custom_call_target="tpu_custom_call" | custom-call | tf_op jit(solution)/shard_map/finish/pallas_call | solution.py:559
